TPU v7x, 256 devices: a whole 4x4x8 slice. The times are simulated.
256 devices in a mesh: dp: 32 (over x, z), mp: 8 (over y, core).
Axes of the slice: x: 4, y: 4, z: 8, core: 2. Of those that a mesh axis runs over, the one named last changes fastest.
Arguments:
- grad_parts: bfloat16 [32, 16, 1024, 1024], P('dp', None, None, 'mp'), may hold values from -6 to 6
- owners: int32 [16], replicated, may hold values from 0 to 7, as said below
- left_stat: float32 [32, 1024, 1024], P('mp', 'dp'), may hold values from -1 to 8
- right_stat: float32 [32, 1024, 1024], P('mp', 'dp'), may hold values from -1 to 8
- left_root: bfloat16 [32, 1024, 1024], P('mp', 'dp'), may hold values from -1 to 9
- right_root: bfloat16 [32, 1024, 1024], P('mp'), may hold values from -1 to 3
- first_moment: float32 [32, 1024, 1024], P('mp', 'dp'), may hold values from -32 to 32
- second_moment: float32 [32, 1024, 1024], P('mp', 'dp'), may hold values from 0.5 to 2
- vec_grad: bfloat16 [32, 73728], P('dp', 'mp'), may hold values from -3 to 3
- vec_first: float32 [73728], P('mp'), may hold values from -4 to 4
- vec_second: float32 [73728], P('mp'), may hold values from 0.5 to 2
Outputs:
- block_update: bfloat16 [16, 1024, 1024], P(None, 'dp', 'mp')
- left_new: float32 [32, 1024, 1024], P('mp', 'dp')
- right_new: float32 [32, 1024, 1024], P('mp', 'dp')
- first_new: float32 [32, 1024, 1024], P('mp', 'dp')
- second_new: float32 [32, 1024, 1024], P('mp', 'dp')
- vec_update: bfloat16 [73728], P('mp')
- vec_first_new: float32 [73728], P('mp')
- vec_second_new: float32 [73728], P('mp')
Inputs may be any that keep to these rules, and one draw needn't show every extreme that they name: `owners`: no owner holds more than 4 blocks, and in every draw some owner holds exactly 4.
All inputs are finite; a program needn't handle non-finite values.
Results may differ from a plain program's by a relative error of at most 0.018.
Values may be sent and summed in bfloat16 or wider, within the bound.
A program may use at most 128 MiB of HBM per device.

v0:
```python
import jax
import jax.numpy as jnp
from jax import lax
from jax.sharding import PartitionSpec as P

beta_one = 0.9
beta_two = 0.95
adam_eps = 1e-08
graft_eps = 1e-06


def owner_table(owners, owner_count, slot_count):
    block_count = owners.shape[0]
    same = owners[:, None] == owners[None, :]
    earlier = lax.broadcasted_iota(jnp.int32, (block_count, block_count), 1) < lax.broadcasted_iota(
        jnp.int32, (block_count, block_count), 0
    )
    slots = jnp.sum((same & earlier).astype(jnp.int32), axis=1)
    owner_ids = lax.broadcasted_iota(jnp.int32, (owner_count, slot_count, block_count), 0)
    slot_ids = lax.broadcasted_iota(jnp.int32, (owner_count, slot_count, block_count), 1)
    return ((owners[None, None, :] == owner_ids) & (slots[None, None, :] == slot_ids)).astype(
        jnp.float32
    )


def body(
    grad_parts,
    owners,
    left_stat,
    right_stat,
    left_root,
    right_root,
    first_moment,
    second_moment,
    vec_grad,
    vec_first,
    vec_second,
):
    owner_count = lax.axis_size("mp")
    slot_count, row_count, order = left_stat.shape
    col_count = order // owner_count
    my_rows = lax.axis_index("dp") * row_count
    my_owner = lax.axis_index("mp")
    row_pieces = lax.psum_scatter(
        grad_parts[0].astype(jnp.float32).astype(jnp.bfloat16),
        "dp",
        scatter_dimension=1,
        tiled=True,
    ).astype(jnp.float32)
    selector = owner_table(owners, owner_count, slot_count)
    outgoing = jnp.einsum("ocb,brw->crow", selector, row_pieces, precision=lax.Precision.HIGHEST)
    incoming = lax.all_to_all(
        outgoing.astype(jnp.bfloat16), "mp", split_axis=2, concat_axis=2, tiled=True
    ).astype(outgoing.dtype)
    grad_rows = incoming.reshape(slot_count, row_count, order)
    mine = lax.dynamic_index_in_dim(selector, my_owner, 0, keepdims=False)
    used_mask = (jnp.sum(mine, axis=1) > 0.5)[:, None, None]
    rounded_rows = grad_rows.astype(jnp.bfloat16)
    shard_rows = lax.all_gather(rounded_rows, "dp", axis=1, tiled=True)
    left_part = jnp.einsum(
        "crk,cnk->crn", rounded_rows, shard_rows, preferred_element_type=jnp.float32
    )
    own_cols = lax.dynamic_slice_in_dim(shard_rows, my_rows, row_count, 2)
    right_acc = jnp.einsum("cnr,cnk->crk", own_cols, shard_rows, preferred_element_type=jnp.float32)
    applied_acc = jnp.einsum(
        "crn,cnk->crk", left_root, shard_rows, preferred_element_type=jnp.float32
    )
    scale = 1.0 / order
    left_new = jnp.where(used_mask, left_stat + left_part * scale, left_stat)
    right_new = jnp.where(used_mask, right_stat + right_acc * scale, right_stat)
    first_new = jnp.where(
        used_mask, beta_one * first_moment + (1.0 - beta_one) * grad_rows, first_moment
    )
    second_new = jnp.where(
        used_mask,
        beta_two * second_moment + (1.0 - beta_two) * grad_rows * grad_rows,
        second_moment,
    )
    adam = first_new / (jnp.sqrt(second_new) + adam_eps)
    precond = jnp.einsum(
        "crk,ckm->crm",
        applied_acc.astype(jnp.bfloat16),
        right_root,
        preferred_element_type=jnp.float32,
    )
    square_adam = jnp.sum(adam * adam, axis=(1, 2))
    square_pre = jnp.sum(precond * precond, axis=(1, 2))
    vec_local = vec_grad[0].astype(jnp.float32)
    square_adam, square_pre, vec_sum = lax.psum((square_adam, square_pre, vec_local), "dp")
    cells = float(order * order)
    graft = jnp.sqrt(square_adam / cells) / jnp.sqrt(square_pre / cells + graft_eps)
    update_rows = (precond * graft[:, None, None]).astype(jnp.bfloat16)
    returned = lax.all_to_all(
        update_rows.reshape(slot_count, row_count, owner_count, col_count),
        "mp",
        split_axis=2,
        concat_axis=2,
        tiled=True,
    )
    block_update = jnp.einsum(
        "ocb,crow->brw", selector.astype(jnp.bfloat16), returned, preferred_element_type=jnp.float32
    ).astype(jnp.bfloat16)
    vec_first_new = beta_one * vec_first + (1.0 - beta_one) * vec_sum
    vec_second_new = beta_two * vec_second + (1.0 - beta_two) * vec_sum * vec_sum
    vec_update = (vec_first_new / (jnp.sqrt(vec_second_new) + adam_eps)).astype(jnp.bfloat16)
    return (
        block_update,
        left_new,
        right_new,
        first_new,
        second_new,
        vec_update,
        vec_first_new,
        vec_second_new,
    )


def solution(mesh):
    placed = (
        P("dp", None, None, "mp"),
        P(),
        P("mp", "dp", None),
        P("mp", "dp", None),
        P("mp", "dp", None),
        P("mp", None, None),
        P("mp", "dp", None),
        P("mp", "dp", None),
        P("dp", "mp"),
        P("mp"),
        P("mp"),
    )
    return jax.shard_map(
        body,
        mesh=mesh,
        in_specs=placed,
        out_specs=(
            P(None, "dp", "mp"),
            P("mp", "dp", None),
            P("mp", "dp", None),
            P("mp", "dp", None),
            P("mp", "dp", None),
            P("mp"),
            P("mp"),
            P("mp"),
        ),
        check_vma=False,
    )
```

profile of v0, /device:TPU:1, one launch (start us, length us, event | category | flops | bytes accessed | tf_op | source)
XLA Modules:
  0.0 519.0 jit_solution(16055392310687253301)
XLA Ops:
  7.2 0.0 copy-start
  7.2 0.0 reduce-scatter.2.cloned.1.call-start
  7.2 0.7 reduce-scatter.2.cloned.1.call-update
  7.9 0.0 all-gather.2.cloned.1.call-start
  8.0 0.9 convert_reduce_fusion
  8.9 224.1 %reduce-scatter.2.cloned.1.call-done = bf16[16,32,128]{2,1,0:T(8,128)(2,1)} async-done(((bf16[16,1024,128]{2,1,0:T(8,128)(2,1)}), bf16[16,32,128]{2,1,0:T(8,128)(2,1)}) %reduce-scatter.2.cloned.1.call-update) | async-done | bytes 131088 | tf_op jit(solution)/shard_map/reduce_scatter | solution.py:44
  233.0 1.1 fusion.4
  234.2 16.5 %all_to_all.10 = bf16[4,32,8,128]{3,1,0,2:T(8,128)(2,1)S(1)} all-to-all(bf16[4,32,8,128]{3,1,0,2:T(8,128)(2,1)S(1)} %copy.31), channel_id=1, replica_groups=mesh['dp'=32,'mp'=8] {'mp'}, dimensions={2} | all-to-all | bytes 524288 | tf_op jit(solution)/shard_map/all_to_all | solution.py:52
  250.7 0.7 copy_bitcast_fusion
  251.4 0.0 all-gather.2.cloned.1.call-update
  251.4 0.8 convert_element_type.50
  252.2 0.7 fusion.19
  252.9 0.1 dynamic-slice_reduce_fusion
  253.0 2.6 multiply_reduce_fusion.1
  255.6 0.0 copy-start.2
  255.6 90.5 %all-gather.2.cloned.1.call-done = bf16[4,1024,1024]{2,1,0:T(8,128)(2,1)} async-done(((bf16[4,32,1024]{2,1,0:T(8,128)(2,1)}), bf16[4,1024,1024]{2,1,0:T(8,128)(2,1)}) %all-gather.2.cloned.1.call-update) | async-done | bytes 8388624 | tf_op jit(solution)/shard_map/all_gather | solution.py:59
  346.1 0.0 copy-done
  346.1 8.9 %multiply_reduce_fusion = (f32[4]{0:T(128)S(1)}, f32[4,32,1024]{2,1,0:T(8,128)S(1)}) fusion(bf16[4,1024,1024]{2,1,0:T(8,128)(2,1)} %param.16, bf16[4,32,1024]{2,1,0:T(8,128)(2,1)S(1)} %copy-done, bf16[4,1024,1024]{2,1,0:T(8,128)(2,1)} %all-gather.2.cloned.1.call-done), kind=kOutput, calls=%fused_computation.20 | convolution fusion | flops 537264128 | bytes 17563664 | tf_op jit(solution)/shard_map/crk,ckm->crm/dot_general | solution.py:80
  355.0 0.0 copy-start.3
  355.0 112.0 %all-reduce = (f32[4]{0:T(128)S(1)}, f32[4]{0:T(128)S(1)}, f32[9216]{0:T(1024)S(1)}) all-reduce(f32[4]{0:T(128)S(1)} %get-tuple-element.41, f32[4]{0:T(128)S(1)} %get-tuple-element.38, f32[9216]{0:T(1024)S(1)} %bitcast.49), channel_id=1, replica_groups=mesh['dp'=32,'mp'=8] {'dp'}, use_global_device_ids=true, to_apply=%region_6.7 | all-reduce | flops 9224 | bytes 73792 | tf_op jit(solution)/shard_map/psum | solution.py:89
  467.0 0.1 multiply_convert_fusion
  467.2 0.9 copy.33
  468.1 32.8 %all-to-all-start.1 = ((bf16[4,32,8,128]{3,0,1,2:T(4,128)(2,1)}), bf16[4,32,8,128]{3,0,1,2:T(4,128)(2,1)S(1)}, u32[]{:S(2)}, u32[]{:S(2)}) async-start(bf16[4,32,8,128]{3,0,1,2:T(4,128)(2,1)} %copy.33), calls=%async_computation.2 | async-start | bytes 524288 | tf_op jit(solution)/shard_map/all_to_all | solution.py:93
  500.9 0.0 copy-done.2
  500.9 0.0 copy-start.1
  500.9 0.0 copy-start.4
  500.9 0.0 copy-start.5
  500.9 0.0 copy-start.6
  501.0 6.9 %fusion.1 = f32[4,32,1024]{2,1,0:T(8,128)} fusion(f32[4,32,1024]{2,1,0:T(8,128)S(1)} %copy-done.2, bf16[4,1024,1024]{2,1,0:T(8,128)(2,1)} %all-gather.2.cloned.1.call-done, pred[4]{0:T(512)(128)(4,1)S(1)} %broadcast_compare_fusion, bf16[4,32,8,128]{3,1,0,2:T(8,128)(2,1)S(1)} %all_to_all.10), kind=kOutput, calls=%fused_computation.3 | convolution fusion | flops 268828672 | bytes 9699332 | tf_op jit(solution)/shard_map/crk,cnk->crn/dot_general | solution.py:60
  507.9 0.0 copy-done.3
  507.9 0.0 copy-done.1
  507.9 2.6 fusion.3
  510.5 0.0 copy-done.4
  510.5 0.0 copy-done.5
  510.5 0.6 divide_convert_fusion
  511.2 0.0 all-to-all-done.1
  511.2 0.0 copy-done.6
  511.2 0.3 fusion.5
  511.4 0.7 copy.36
  (4 shorter events, 0.1 us)
Async XLA Ops:
  7.2 338.9 %copy-start = (bf16[4,32,1024]{2,1,0:T(8,128)(2,1)S(1)}, bf16[4,32,1024]{2,1,0:T(8,128)(2,1)}, u32[]{:S(2)}) copy-start(bf16[4,32,1024]{2,1,0:T(8,128)(2,1)} %param.15) | copy-start | bytes 786436
  7.2 225.8 %reduce-scatter.2.cloned.1.call-start = ((), (), s32[]{:S(2)}) async-start(), calls=%async_computation.3 | async-start | bytes 4325376 | tf_op jit(solution)/shard_map/reduce_scatter | solution.py:44
  7.9 338.2 %all-gather.2.cloned.1.call-start = ((), (), s32[]{:S(2)}) async-start(), calls=%async_computation.4 | async-start | bytes 8650752 | tf_op jit(solution)/shard_map/all_gather | solution.py:59
  255.6 245.3 %copy-start.2 = (f32[4,32,1024]{2,1,0:T(8,128)S(1)}, f32[4,32,1024]{2,1,0:T(8,128)}, u32[]{:S(2)}) copy-start(f32[4,32,1024]{2,1,0:T(8,128)} %param.13) | copy-start | bytes 1572868
  355.0 152.9 %copy-start.3 = (f32[4,32,1024]{2,1,0:T(8,128)S(1)}, f32[4,32,1024]{2,1,0:T(8,128)}, u32[]{:S(2)}) copy-start(f32[4,32,1024]{2,1,0:T(8,128)} %param.14) | copy-start | bytes 1572868
  468.1 43.1 %all-to-all-start.1 = ((bf16[4,32,8,128]{3,0,1,2:T(4,128)(2,1)}), bf16[4,32,8,128]{3,0,1,2:T(4,128)(2,1)S(1)}, u32[]{:S(2)}, u32[]{:S(2)}) async-start(bf16[4,32,8,128]{3,0,1,2:T(4,128)(2,1)} %copy.33), calls=%async_computation.2 | async-start | bytes 524288 | tf_op jit(solution)/shard_map/all_to_all | solution.py:93
  500.9 7.0 %copy-start.1 = (bf16[4,1024,1024]{2,1,0:T(8,128)(2,1)S(1)}, bf16[4,1024,1024]{2,1,0:T(8,128)(2,1)}, u32[]{:S(2)}) copy-start(bf16[4,1024,1024]{2,1,0:T(8,128)(2,1)} %all-gather.2.cloned.1.call-done) | copy-start | bytes 25165828
  500.9 9.6 %copy-start.4 = (f32[9216]{0:T(1024)S(1)}, f32[9216]{0:T(1024)}, u32[]{:S(2)}) copy-start(f32[9216]{0:T(1024)} %param.21) | copy-start | bytes 110596
  500.9 9.6 %copy-start.5 = (f32[9216]{0:T(1024)S(1)}, f32[9216]{0:T(1024)}, u32[]{:S(2)}) copy-start(f32[9216]{0:T(1024)} %param.20) | copy-start | bytes 110596
  500.9 10.2 %copy-start.6 = (s32[16]{0:T(128)S(1)}, s32[16]{0:T(128)}, u32[]{:S(2)}) copy-start(s32[16]{0:T(128)} %param.12) | copy-start | bytes 196
Sparse Core Ops, SparseCore 0:
  11.9 221.0 reduce-scatter.1
  251.5 94.4 all-gather.1
where the time goes:
time: 519 us
  waiting for transfers between devices  315 us (61%)
  blocking collectives  129 us (25%)
  starting transfers between devices  32.9 us (6%)
  matrix products  19.8 us (4%)
  between operations  14.1 us (3%)
  other arithmetic  5.83 us (1%)
    reduce_scatter x1, waiting for transfers between devices, body(): lax.psum_scatter(grad_parts[0].astype(jnp.float32).astype(jnp.bfloat16),...  224 us
    psum x1, blocking collectives, body(): lax.psum((square_adam, square_pre, vec_local), 'dp')  112 us
    all_gather x1, waiting for transfers between devices, body(): shard_rows = lax.all_gather(rounded_rows, 'dp', axis=1, tiled=True)  90.5 us
    all_to_all x1, starting transfers between devices, body(): lax.all_to_all(update_rows.reshape(slot_count, row_count, owner_count, co...  32.8 us
    all_to_all x1, blocking collectives, body(): lax.all_to_all(outgoing.astype(jnp.bfloat16), 'mp', split_axis=2, concat_...  16.5 us
  transfers between devices with their start and end apart: 3, of which 2 were waited for; matrix products, arithmetic and copies ran while one was open for 3% of the time, Pallas kernels for 0%

commit v1 on v0

--- a/solution.py
+++ b/solution.py
@@ -7,6 +7,9 @@
 beta_two = 0.95
 adam_eps = 1e-08
 graft_eps = 1e-06
+_fit_entries = lambda row_data: jnp.concatenate(
+    lax.all_to_all(jnp.stack([row_data for _ in range(lax.psum(1, "dp"))], axis=0), "dp", 0, 0), 1
+)
 
 
 def owner_table(owners, owner_count, slot_count):
@@ -56,7 +59,7 @@
     mine = lax.dynamic_index_in_dim(selector, my_owner, 0, keepdims=False)
     used_mask = (jnp.sum(mine, axis=1) > 0.5)[:, None, None]
     rounded_rows = grad_rows.astype(jnp.bfloat16)
-    shard_rows = lax.all_gather(rounded_rows, "dp", axis=1, tiled=True)
+    shard_rows = _fit_entries(rounded_rows)
     left_part = jnp.einsum(
         "crk,cnk->crn", rounded_rows, shard_rows, preferred_element_type=jnp.float32
     )

time: 519 us -> 638 us (1.23)
  waiting for transfers between devices: 315 us -> 408 us
  starting transfers between devices: 32.9 us -> 46 us
  local copies, waits for them, and re-layouts: 2.49 us -> 14.5 us
    all_to_all x0 -> x1, waiting for transfers between devices: none -> 183 us  [lax.all_to_all(jnp.stack([row_data for _ in range(lax.psum(1, 'dp'))], ax...]
    all_gather x1 -> x0, waiting for transfers between devices: 90.5 us -> none  [body(): shard_rows = lax.all_gather(rounded_rows, 'dp', axis=1, tiled=True)]
    reshape x0 -> x1, local copies, waits for them, and re-layouts: none -> 8.47 us  [jnp.concatenate(lax.all_to_all(jnp.stack([row_data for _ in range(lax.psu...]
    all_to_all x0 -> x1, starting transfers between devices: none -> 6.63 us  [lax.all_to_all(jnp.stack([row_data for _ in range(lax.psum(1, 'dp'))], ax...]
    all_to_all x1, starting transfers between devices: 32.8 us -> 39.3 us  [body(): lax.all_to_all(update_rows.reshape(slot_count, row_count, owner_count, co...]
  transfers between devices with their start and end apart: 3 -> 3, of which waited for: 2 -> 2; matrix products, arithmetic and copies ran while one was open for 3% -> 2% of each run, Pallas kernels for 0% -> 0%
where the time goes in v1:
time: 638 us
  waiting for transfers between devices  408 us (64%)
  blocking collectives  131 us (21%)
  starting transfers between devices  46 us (7%)
  matrix products  20.2 us (3%)
  local copies, waits for them, and re-layouts  14.5 us (2%)
  between operations  14.2 us (2%)
    reduce_scatter x1, waiting for transfers between devices, body(): lax.psum_scatter(grad_parts[0].astype(jnp.float32).astype(jnp.bfloat16),...  224 us
    all_to_all x1, waiting for transfers between devices, lax.all_to_all(jnp.stack([row_data for _ in range(lax.psum(1, 'dp'))], ax...  183 us
    psum x1, blocking collectives, body(): lax.psum((square_adam, square_pre, vec_local), 'dp')  115 us
    all_to_all x1, starting transfers between devices, body(): lax.all_to_all(update_rows.reshape(slot_count, row_count, owner_count, co...  39.3 us
    all_to_all x1, blocking collectives, body(): lax.all_to_all(outgoing.astype(jnp.bfloat16), 'mp', split_axis=2, concat_...  16.5 us
  transfers between devices with their start and end apart: 3, of which 2 were waited for; matrix products, arithmetic and copies ran while one was open for 2% of the time, Pallas kernels for 0%

profile of v1, /device:TPU:1, one launch (start us, length us, event | category | flops | bytes accessed | tf_op | source)
XLA Modules:
  0.0 637.6 jit_solution(17236100801124281360)
XLA Ops:
  7.2 0.0 copy-start
  7.2 0.0 reduce-scatter.2.cloned.1.call-start
  7.2 0.7 reduce-scatter.2.cloned.1.call-update
  7.9 0.9 convert_reduce_fusion
  8.8 224.1 %reduce-scatter.2.cloned.1.call-done = bf16[16,32,128]{2,1,0:T(8,128)(2,1)} async-done(((bf16[16,1024,128]{2,1,0:T(8,128)(2,1)}), bf16[16,32,128]{2,1,0:T(8,128)(2,1)}) %reduce-scatter.2.cloned.1.call-update) | async-done | bytes 131088 | tf_op jit(solution)/shard_map/reduce_scatter | solution.py:47
  233.0 1.1 fusion.4
  234.2 16.5 %all_to_all.15 = bf16[4,32,8,128]{3,1,0,2:T(8,128)(2,1)S(1)} all-to-all(bf16[4,32,8,128]{3,1,0,2:T(8,128)(2,1)S(1)} %copy.32), channel_id=1, replica_groups=mesh['dp'=32,'mp'=8] {'mp'}, dimensions={2} | all-to-all | bytes 524288 | tf_op jit(solution)/shard_map/all_to_all | solution.py:55
  250.7 4.3 stack.2
  255.0 0.0 copy-start.8
  255.0 0.0 copy-start.9
  255.0 0.0 copy-start.3
  255.0 0.0 copy-start.4
  255.0 6.6 %all-to-all-start.1 = ((bf16[32,4,32,1024]{3,2,1,0:T(8,128)(2,1)}), bf16[32,4,32,1024]{3,2,1,0:T(8,128)(2,1)}, u32[]{:S(2)}, u32[]{:S(2)}) async-start(bf16[32,4,32,1024]{3,2,1,0:T(8,128)(2,1)} %stack.2), calls=%async_computation.2 | async-start | bytes 16777216 | tf_op jit(solution)/shard_map/all_to_all | solution.py:11
  261.6 0.0 copy-done.8
  261.7 0.0 copy-done.9
  261.7 0.1 dynamic-slice_reduce_fusion
  261.9 0.0 copy-done.3
  261.9 0.0 copy-done.4
  261.9 1.4 multiply_reduce_fusion.1
  263.2 183.4 %all-to-all-done.1 = bf16[32,4,32,1024]{3,2,1,0:T(8,128)(2,1)} async-done(((bf16[32,4,32,1024]{3,2,1,0:T(8,128)(2,1)}), bf16[32,4,32,1024]{3,2,1,0:T(8,128)(2,1)}, u32[]{:S(2)}, u32[]{:S(2)}) %all-to-all-start.1) | async-done | bytes 8388640 | tf_op jit(solution)/shard_map/all_to_all | solution.py:11
  446.6 8.5 %copy.34 = bf16[4,32,32,1024]{3,2,1,0:T(8,128)(2,1)} copy(bf16[4,32,32,1024]{3,2,0,1:T(8,128)(2,1)} %bitcast.6) | data formatting | bytes 16777216 | tf_op jit(solution)/shard_map/reshape | solution.py:10
  455.1 0.0 copy-done
  455.1 0.0 copy-start.5
  455.1 8.9 %multiply_reduce_fusion = (f32[4]{0:T(128)S(1)}, f32[4,32,1024]{2,1,0:T(8,128)S(1)}) fusion(bf16[4,1024,1024]{2,1,0:T(8,128)(2,1)} %param.16, bf16[4,32,1024]{2,1,0:T(8,128)(2,1)S(1)} %copy-done, bf16[4,1024,1024]{2,1,0:T(8,128)(2,1)} %bitcast.48), kind=kOutput, calls=%fused_computation.20 | convolution fusion | flops 537264128 | bytes 17563664 | tf_op jit(solution)/shard_map/crk,ckm->crm/dot_general | solution.py:83
  464.0 0.0 copy-start.2
  464.0 114.8 %all-reduce = (f32[4]{0:T(128)S(1)}, f32[4]{0:T(128)S(1)}, f32[9216]{0:T(1024)S(1)}) all-reduce(f32[4]{0:T(128)S(1)} %get-tuple-element.41, f32[4]{0:T(128)S(1)} %get-tuple-element.38, f32[9216]{0:T(1024)S(1)} %bitcast.54), channel_id=1, replica_groups=mesh['dp'=32,'mp'=8] {'dp'}, use_global_device_ids=true, to_apply=%region_6.7 | all-reduce | flops 9224 | bytes 73792 | tf_op jit(solution)/shard_map/psum | solution.py:92
  578.8 0.1 multiply_convert_fusion
  579.0 0.9 copy.35
  579.9 39.3 %all-to-all-start.2 = ((bf16[4,32,8,128]{3,0,1,2:T(4,128)(2,1)}), bf16[4,32,8,128]{3,0,1,2:T(4,128)(2,1)S(1)}, u32[]{:S(2)}, u32[]{:S(2)}) async-start(bf16[4,32,8,128]{3,0,1,2:T(4,128)(2,1)} %copy.35), calls=%async_computation.3 | async-start | bytes 524288 | tf_op jit(solution)/shard_map/all_to_all | solution.py:96
  619.2 0.0 copy-done.5
  619.2 0.0 copy-start.1
  619.2 0.0 copy-start.6
  619.2 0.0 copy-start.7
  619.2 6.5 %fusion.3 = f32[4,32,1024]{2,1,0:T(8,128)} fusion(f32[4,32,1024]{2,1,0:T(8,128)S(1)} %copy-done.5, bf16[4,1024,1024]{2,1,0:T(8,128)(2,1)} %bitcast.49, s32[]{:T(128)S(6)} %select_n.24, pred[4]{0:T(512)(128)(4,1)S(1)} %broadcast_compare_fusion), kind=kOutput, calls=%fused_computation.5 | convolution fusion | flops 268828672 | bytes 10485768 | tf_op jit(solution)/shard_map/cnr,cnk->crk/dot_general | solution.py:67
  625.7 0.0 copy-done.2
  625.7 0.0 copy-done.1
  625.7 3.4 fusion.1
  629.1 0.0 copy-done.6
  629.1 0.0 copy-done.7
  629.1 0.6 divide_convert_fusion
  629.8 0.0 all-to-all-done.2
  629.8 0.3 fusion.5
  630.0 0.7 copy.38
  (7 shorter events, 0.2 us)
Async XLA Ops:
  7.2 447.9 %copy-start = (bf16[4,32,1024]{2,1,0:T(8,128)(2,1)S(1)}, bf16[4,32,1024]{2,1,0:T(8,128)(2,1)}, u32[]{:S(2)}) copy-start(bf16[4,32,1024]{2,1,0:T(8,128)(2,1)} %param.15) | copy-start | bytes 786436
  7.2 225.8 %reduce-scatter.2.cloned.1.call-start = ((), (), s32[]{:S(2)}) async-start(), calls=%async_computation.4 | async-start | bytes 4325376 | tf_op jit(solution)/shard_map/reduce_scatter | solution.py:47
  255.0 6.7 %copy-start.8 = (bf16[1,9216]{1,0:T(2,128)(2,1)S(1)}, bf16[1,9216]{1,0:T(2,128)(2,1)}, u32[]{:S(2)}) copy-start(bf16[1,9216]{1,0:T(2,128)(2,1)} %param.19) | copy-start | bytes 55300
  255.0 6.7 %copy-start.9 = (s32[16]{0:T(128)S(1)}, s32[16]{0:T(128)}, u32[]{:S(2)}) copy-start(s32[16]{0:T(128)} %param.12) | copy-start | bytes 196
  255.0 6.9 %copy-start.3 = (f32[4,32,1024]{2,1,0:T(8,128)S(1)}, f32[4,32,1024]{2,1,0:T(8,128)}, u32[]{:S(2)}) copy-start(f32[4,32,1024]{2,1,0:T(8,128)} %param.18) | copy-start | bytes 1572868
  255.0 6.9 %copy-start.4 = (f32[4,32,1024]{2,1,0:T(8,128)S(1)}, f32[4,32,1024]{2,1,0:T(8,128)}, u32[]{:S(2)}) copy-start(f32[4,32,1024]{2,1,0:T(8,128)} %param.17) | copy-start | bytes 1572868
  255.0 191.6 %all-to-all-start.1 = ((bf16[32,4,32,1024]{3,2,1,0:T(8,128)(2,1)}), bf16[32,4,32,1024]{3,2,1,0:T(8,128)(2,1)}, u32[]{:S(2)}, u32[]{:S(2)}) async-start(bf16[32,4,32,1024]{3,2,1,0:T(8,128)(2,1)} %stack.2), calls=%async_computation.2 | async-start | bytes 16777216 | tf_op jit(solution)/shard_map/all_to_all | solution.py:11
  455.1 164.1 %copy-start.5 = (f32[4,32,1024]{2,1,0:T(8,128)S(1)}, f32[4,32,1024]{2,1,0:T(8,128)}, u32[]{:S(2)}) copy-start(f32[4,32,1024]{2,1,0:T(8,128)} %param.14) | copy-start | bytes 1572868
  464.0 161.7 %copy-start.2 = (f32[4,32,1024]{2,1,0:T(8,128)S(1)}, f32[4,32,1024]{2,1,0:T(8,128)}, u32[]{:S(2)}) copy-start(f32[4,32,1024]{2,1,0:T(8,128)} %param.13) | copy-start | bytes 1572868
  579.9 49.9 %all-to-all-start.2 = ((bf16[4,32,8,128]{3,0,1,2:T(4,128)(2,1)}), bf16[4,32,8,128]{3,0,1,2:T(4,128)(2,1)S(1)}, u32[]{:S(2)}, u32[]{:S(2)}) async-start(bf16[4,32,8,128]{3,0,1,2:T(4,128)(2,1)} %copy.35), calls=%async_computation.3 | async-start | bytes 524288 | tf_op jit(solution)/shard_map/all_to_all | solution.py:96
  619.2 6.5 %copy-start.1 = (bf16[4,32,32,1024]{3,2,1,0:T(8,128)(2,1)S(1)}, bf16[4,32,32,1024]{3,2,1,0:T(8,128)(2,1)}, u32[]{:S(2)}) copy-start(bf16[4,32,32,1024]{3,2,1,0:T(8,128)(2,1)} %copy.34) | copy-start | bytes 25165828
  619.2 9.9 %copy-start.6 = (f32[9216]{0:T(1024)S(1)}, f32[9216]{0:T(1024)}, u32[]{:S(2)}) copy-start(f32[9216]{0:T(1024)} %param.21) | copy-start | bytes 110596
  619.2 9.9 %copy-start.7 = (f32[9216]{0:T(1024)S(1)}, f32[9216]{0:T(1024)}, u32[]{:S(2)}) copy-start(f32[9216]{0:T(1024)} %param.20) | copy-start | bytes 110596
Sparse Core Ops, SparseCore 0:
  11.9 221.0 reduce-scatter.1
